TPU v7x, 32 devices: a whole 2x2x4 slice. The times are simulated.
32 devices in a mesh: row: 2 (over y), col: 16 (over z, x, core).
Axes of the slice: x: 2, y: 2, z: 4, core: 2. Of those that a mesh axis runs over, the one named last changes fastest.
Arguments:
- w_slab: float32 [512, 16384], P('row', 'col'), may hold values from -0.25 to 0.25
- prior_cov: float32 [16384, 16384], P('row', 'col'), as said below
Outputs:
- posterior: float32 [16384, 16384], P('row', 'col')
Inputs may be any that keep to these rules, and one draw needn't show every extreme that they name: prior_cov is symmetric.
All inputs are finite; a program needn't handle non-finite values.
Results may differ from a plain program's by a relative error of at most 0.00005.
Values sent between devices are 32-bit elements; how exact they have to be, the bound alone decides.
No kernel may reach another device: no remote copies, remote signals or barrier semaphores. Data moves between devices by JAX's collectives and lax.ppermute only.
A program may use at most 256 MiB of HBM per device.

v0:
```python
import jax
import jax.numpy as jnp
from jax import lax
from jax.sharding import PartitionSpec as P


def from_root(value, axis, source):
    kept = jnp.where(lax.axis_index(axis) == source, value, 0).astype(value.dtype)
    return lax.psum(kept, axis)


def shards(w_slab, prior_cov):
    own_block = lax.all_gather(w_slab, "row", axis=0, tiled=True)
    width = own_block.shape[1]
    groups = lax.axis_size("col") // lax.axis_size("row")
    row_index = lax.axis_index("row")
    result = prior_cov
    for step in range(groups):
        slot = jnp.int32(step)
        root = row_index * groups + slot
        received = from_root(own_block, "col", root)
        product = lax.dot_general(
            received,
            own_block,
            (((0,), (0,)), ((), ())),
            precision=lax.Precision.HIGHEST,
            preferred_element_type=jnp.float32,
        )
        start = slot * width
        current = lax.dynamic_slice_in_dim(result, start, width, 0)
        result = lax.dynamic_update_slice_in_dim(result, current - product, start, 0)
    return result


def solution(mesh):
    return jax.shard_map(
        shards,
        mesh=mesh,
        in_specs=(P("row", "col"), P("row", "col")),
        out_specs=P("row", "col"),
        check_vma=False,
    )
```

profile of v0, /device:TPU:0, one launch (start us, length us, event | category | flops | bytes accessed | tf_op | source)
XLA Modules:
  0.0 460.4 jit_solution(723718083218252764)
XLA Ops:
  6.5 0.0 all-gather.2.cloned.1.call-start
  6.5 23.5 %copy.20 = f32[8192,1024]{1,0:T(8,128)} copy(f32[8192,1024]{1,0:T(8,128)} %param.3) | data formatting | bytes 67108864
  30.0 0.0 all-gather.2.cloned.1.call-update
  30.0 0.0 all-reduce.3.cloned.1.call-start
  30.1 35.9 %all-gather.2.cloned.1.call-done = f32[512,1024]{1,0:T(8,128)} async-done(((f32[256,1024]{1,0:T(8,128)}), f32[512,1024]{1,0:T(8,128)}) %all-gather.2.cloned.1.call-update) | async-done | bytes 2097168 | tf_op jit(solution)/shard_map/all_gather | solution.py:13
  66.0 7.8 %broadcast_select_fusion = (f32[512,1024]{1,0:T(8,128)}, f32[512,1024]{1,0:T(8,128)}, f32[512,1024]{1,0:T(8,128)}, f32[512,1024]{1,0:T(8,128)}, f32[512,1024]{1,...) fusion(f32[512,1024]{1,0:T(8,128)} %all-gather.2.cloned.1.call-done, pred[]{:T(512)S(6)} %eq.31, ...), kind=kLoop, calls=%fused_computation.15 | loop fusion | flops 4194304 | bytes 18874376 | tf_op jit(solution)/shard_map/jit(_where)/select_n | solution.py:8
  73.8 0.0 copy-start
  73.8 0.0 all-reduce.3.cloned.1.call-update
  73.9 298.4 %all-reduce.3.cloned.1.call-done = (f32[512,1024]{1,0:T(8,128)}, f32[512,1024]{1,0:T(8,128)}, f32[512,1024]{1,0:T(8,128)}, f32[512,1024]{1,0:T(8,128)}, f32[512,...) async-done(((f32[512,1024]{1,0:T(8,128)}, f32[512,1024]{1,0:T(8,128)}, f32[512,1024]{1,0:T(8,128)}, f32[512,1024]{1,0:T(8,128)}, ...) | async-done | bytes 16777232 | tf_op jit(solution)/shard_map/psum | solution.py:9
  372.3 0.0 copy-done
  372.3 0.0 copy-start.7
  372.3 10.4 %subtract_dynamic-update-slice_fusion = f32[8192,1024]{1,0:T(8,128)} fusion(f32[8192,1024]{1,0:T(8,128)} %copy.20, f32[512,1024]{1,0:T(8,128)} %get-tuple-element.5, f32[512,1024]{1,0:T(8,128)S(1)} %copy-done), kind=kOutput, calls=%fused_computation.14 | convolution fusion | flops 6443499520 | bytes 12582912 | tf_op jit(solution)/shard_map/dot_general | solution.py:22
  382.7 0.0 copy-done.7
  382.7 0.0 copy-start.6
  382.7 10.1 %fusion.6 = f32[8192,1024]{1,0:T(8,128)} fusion(f32[8192,1024]{1,0:T(8,128)} %subtract_dynamic-update-slice_fusion, f32[512,1024]{1,0:T(8,128)S(1)} %copy-done.7, f32[512,1024]{1,0:T(8,128)S(1)} %copy-done), kind=kOutput, calls=%fused_computation.13 | convolution fusion | flops 6443499520 | bytes 12582912 | tf_op jit(solution)/shard_map/dot_general | solution.py:22
  392.8 0.0 copy-done.6
  392.8 0.0 copy-start.5
  392.8 10.1 %fusion.5 = f32[8192,1024]{1,0:T(8,128)} fusion(f32[8192,1024]{1,0:T(8,128)} %fusion.6, f32[512,1024]{1,0:T(8,128)S(1)} %copy-done.6, f32[512,1024]{1,0:T(8,128)S(1)} %copy-done), kind=kOutput, calls=%fused_computation.11 | convolution fusion | flops 6443499520 | bytes 12582912 | tf_op jit(solution)/shard_map/dot_general | solution.py:22
  402.9 0.0 copy-done.5
  402.9 0.0 copy-start.4
  402.9 10.2 %fusion.4 = f32[8192,1024]{1,0:T(8,128)} fusion(f32[8192,1024]{1,0:T(8,128)} %fusion.5, f32[512,1024]{1,0:T(8,128)S(1)} %copy-done.5, f32[512,1024]{1,0:T(8,128)S(1)} %copy-done), kind=kOutput, calls=%fused_computation.9 | convolution fusion | flops 6443499520 | bytes 12582912 | tf_op jit(solution)/shard_map/dot_general | solution.py:22
  413.1 0.0 copy-done.4
  413.1 0.0 copy-start.3
  413.1 10.1 %fusion.3 = f32[8192,1024]{1,0:T(8,128)} fusion(f32[8192,1024]{1,0:T(8,128)} %fusion.4, f32[512,1024]{1,0:T(8,128)S(1)} %copy-done.4, f32[512,1024]{1,0:T(8,128)S(1)} %copy-done), kind=kOutput, calls=%fused_computation.7 | convolution fusion | flops 6443499520 | bytes 12582912 | tf_op jit(solution)/shard_map/dot_general | solution.py:22
  423.2 0.0 copy-done.3
  423.2 0.0 copy-start.2
  423.2 10.1 %fusion.2 = f32[8192,1024]{1,0:T(8,128)} fusion(f32[8192,1024]{1,0:T(8,128)} %fusion.3, f32[512,1024]{1,0:T(8,128)S(1)} %copy-done.3, f32[512,1024]{1,0:T(8,128)S(1)} %copy-done), kind=kOutput, calls=%fused_computation.5 | convolution fusion | flops 6443499520 | bytes 12582912 | tf_op jit(solution)/shard_map/dot_general | solution.py:22
  433.3 0.0 copy-done.2
  433.3 0.0 copy-start.1
  433.3 10.3 %fusion.1 = f32[8192,1024]{1,0:T(8,128)} fusion(f32[8192,1024]{1,0:T(8,128)} %fusion.2, f32[512,1024]{1,0:T(8,128)S(1)} %copy-done.2, f32[512,1024]{1,0:T(8,128)S(1)} %copy-done), kind=kOutput, calls=%fused_computation.3 | convolution fusion | flops 6443499520 | bytes 12582912 | tf_op jit(solution)/shard_map/dot_general | solution.py:22
  443.6 0.0 copy-done.1
  443.6 9.9 %fusion = f32[8192,1024]{1,0:T(8,128)} fusion(f32[8192,1024]{1,0:T(8,128)} %fusion.1, f32[512,1024]{1,0:T(8,128)S(1)} %copy-done.1, f32[512,1024]{1,0:T(8,128)S(1)} %copy-done), kind=kOutput, calls=%fused_computation.1 | convolution fusion | flops 6443499520 | bytes 12582912 | tf_op jit(solution)/shard_map/dot_general | solution.py:22
Async XLA Ops:
  6.5 59.5 %all-gather.2.cloned.1.call-start = ((), (), s32[]{:S(2)}) async-start(), calls=%async_computation | async-start | bytes 3145728 | tf_op jit(solution)/shard_map/all_gather | solution.py:13
  30.0 342.3 %all-reduce.3.cloned.1.call-start = ((), (), s32[]{:S(2)}) async-start(), calls=%async_computation.1 | async-start | bytes 33554432 | tf_op jit(solution)/shard_map/psum | solution.py:9
  73.8 298.5 %copy-start = (f32[512,1024]{1,0:T(8,128)S(1)}, f32[512,1024]{1,0:T(8,128)}, u32[]{:S(2)}) copy-start(f32[512,1024]{1,0:T(8,128)} %all-gather.2.cloned.1.call-done) | copy-start | bytes 6291460
  372.3 10.4 %copy-start.7 = (f32[512,1024]{1,0:T(8,128)S(1)}, f32[512,1024]{1,0:T(8,128)}, u32[]{:S(2)}) copy-start(f32[512,1024]{1,0:T(8,128)} %get-tuple-element.6) | copy-start | bytes 6291460
  382.7 10.1 %copy-start.6 = (f32[512,1024]{1,0:T(8,128)S(1)}, f32[512,1024]{1,0:T(8,128)}, u32[]{:S(2)}) copy-start(f32[512,1024]{1,0:T(8,128)} %get-tuple-element.7) | copy-start | bytes 6291460
  392.8 10.1 %copy-start.5 = (f32[512,1024]{1,0:T(8,128)S(1)}, f32[512,1024]{1,0:T(8,128)}, u32[]{:S(2)}) copy-start(f32[512,1024]{1,0:T(8,128)} %get-tuple-element.8) | copy-start | bytes 6291460
  402.9 10.2 %copy-start.4 = (f32[512,1024]{1,0:T(8,128)S(1)}, f32[512,1024]{1,0:T(8,128)}, u32[]{:S(2)}) copy-start(f32[512,1024]{1,0:T(8,128)} %get-tuple-element.9) | copy-start | bytes 6291460
  413.1 10.1 %copy-start.3 = (f32[512,1024]{1,0:T(8,128)S(1)}, f32[512,1024]{1,0:T(8,128)}, u32[]{:S(2)}) copy-start(f32[512,1024]{1,0:T(8,128)} %get-tuple-element.10) | copy-start | bytes 6291460
  423.2 10.1 %copy-start.2 = (f32[512,1024]{1,0:T(8,128)S(1)}, f32[512,1024]{1,0:T(8,128)}, u32[]{:S(2)}) copy-start(f32[512,1024]{1,0:T(8,128)} %get-tuple-element.11) | copy-start | bytes 6291460
  433.3 10.3 %copy-start.1 = (f32[512,1024]{1,0:T(8,128)S(1)}, f32[512,1024]{1,0:T(8,128)}, u32[]{:S(2)}) copy-start(f32[512,1024]{1,0:T(8,128)} %get-tuple-element.12) | copy-start | bytes 6291460
Sparse Core Ops, SparseCore 0:
  30.1 35.8 all-gather.1
  74.0 298.2 all-reduce.2
where the time goes:
time: 461 us; the launch traced here: 460 us
  waiting for transfers between devices  334 us (72%)
  matrix products  81.2 us (18%)
  local copies, waits for them, and re-layouts  23.5 us (5%)
  between operations  13.4 us (3%)
  other arithmetic  7.85 us (2%)
    psum x1, waiting for transfers between devices, from_root(): return lax.psum(kept, axis)  298 us
    dot_general x8, matrix products, shards(): lax.dot_general(received, own_block, (((0,), (0,)), ((), ())), precision=...  81.2 us
    all_gather x1, waiting for transfers between devices, shards(): own_block = lax.all_gather(w_slab, 'row', axis=0, tiled=True)  35.9 us
    unnamed x17, local copies, waits for them, and re-layouts  23.5 us
  transfers between devices with their start and end apart: 2, of which 2 were waited for; matrix products, arithmetic and copies ran while one was open for 0% of the time, Pallas kernels for 0%

commit v1 on v0

--- a/solution.py
+++ b/solution.py
@@ -10,7 +10,17 @@
 
 
 def shards(w_slab, prior_cov):
-    own_block = lax.all_gather(w_slab, "row", axis=0, tiled=True)
+    after = lax.psum(1, "row")
+    x_next = lax.axis_index("row")
+    f_now, k_now, new = (after, x_next, w_slab.shape[0])
+    value_now, far_arr = (w_slab, 1)
+    while far_arr < f_now:
+        view_out = lax.ppermute(
+            value_now, "row", perm=[(idx, (idx - far_arr) % f_now) for idx in range(f_now)]
+        )
+        value_now = jnp.concatenate([value_now, view_out], axis=0)
+        far_arr = 2 * far_arr
+    own_block = jnp.roll(value_now, k_now * new, axis=0)
     width = own_block.shape[1]
     groups = lax.axis_size("col") // lax.axis_size("row")
     row_index = lax.axis_index("row")

time: 461 us -> 454 us (0.985)
  waiting for transfers between devices: 334 us -> 323 us
    all_gather x1 -> x0, waiting for transfers between devices: 35.9 us -> none  [shards(): own_block = lax.all_gather(w_slab, 'row', axis=0, tiled=True)]
    ppermute x0 -> x1, waiting for transfers between devices: none -> 23.3 us  [shards(): lax.ppermute(value_now, 'row', perm=[(idx, (idx - far_arr) % f_now) for i...]
    select_n x1 -> x2, other arithmetic: 7.85 us -> 9.35 us  [from_root(): jnp.where(lax.axis_index(axis) == source, value, 0).astype(value.dtype)]
where the time goes in v1:
time: 454 us
  waiting for transfers between devices  323 us (71%)
  matrix products  81.2 us (18%)
  local copies, waits for them, and re-layouts  23.6 us (5%)
  between operations  13.4 us (3%)
  other arithmetic  9.35 us (2%)
    psum x1, waiting for transfers between devices, from_root(): return lax.psum(kept, axis)  300 us
    dot_general x8, matrix products, shards(): lax.dot_general(received, own_block, (((0,), (0,)), ((), ())), precision=...  81.2 us
    unnamed x17, local copies, waits for them, and re-layouts  23.6 us
    ppermute x1, waiting for transfers between devices, shards(): lax.ppermute(value_now, 'row', perm=[(idx, (idx - far_arr) % f_now) for i...  23.3 us
    select_n x2, other arithmetic, from_root(): jnp.where(lax.axis_index(axis) == source, value, 0).astype(value.dtype)  9.35 us
  transfers between devices with their start and end apart: 2, of which 2 were waited for; matrix products, arithmetic and copies ran while one was open for 0% of the time, Pallas kernels for 0%

profile of v1, /device:TPU:0, one launch (start us, length us, event | category | flops | bytes accessed | tf_op | source)
XLA Modules:
  0.0 453.7 jit_solution(9018871552728309801)
XLA Ops:
  6.5 0.0 copy-start.7
  6.5 0.0 all-reduce.3.cloned.1.call-start
  6.5 23.5 %copy.20 = f32[8192,1024]{1,0:T(8,128)} copy(f32[8192,1024]{1,0:T(8,128)} %param.3) | data formatting | bytes 67108864
  30.1 0.0 copy-done.7
  30.1 3.0 collective-permute-start
  33.1 23.3 %collective-permute-done = f32[256,1024]{1,0:T(8,128)} collective-permute-done((f32[256,1024]{1,0:T(8,128)S(1)}, f32[256,1024]{1,0:T(8,128)}, u32[]{:S(2)}, u32[]{:S(2)}) %collective-permute-start) | collective-permute-done | bytes 1048608 | tf_op jit(solution)/shard_map/ppermute | solution.py:18
  56.3 4.0 broadcast_select_fusion
  60.3 5.4 %broadcast_select_fusion.1 = (f32[512,1024]{1,0:T(8,128)}, f32[512,1024]{1,0:T(8,128)}, f32[512,1024]{1,0:T(8,128)}, f32[512,1024]{1,0:T(8,128)}, f32[512,1024]{...) fusion(f32[512,1024]{1,0:T(8,128)S(1)} %get-tuple-element.14, pred[]{:T(512)S(6)} %eq.33, pred[]{:T(512)S(6)} %eq.32, ...), kind=kLoop, calls=%fused_computation.23 | loop fusion | flops 3670016 | bytes 16777224 | tf_op jit(solution)/shard_map/jit(_where)/select_n | solution.py:8
  65.7 0.0 all-reduce.3.cloned.1.call-update
  65.7 299.9 %all-reduce.3.cloned.1.call-done = (f32[512,1024]{1,0:T(8,128)}, f32[512,1024]{1,0:T(8,128)}, f32[512,1024]{1,0:T(8,128)}, f32[512,1024]{1,0:T(8,128)}, f32[512,...) async-done(((f32[512,1024]{1,0:T(8,128)}, f32[512,1024]{1,0:T(8,128)}, f32[512,1024]{1,0:T(8,128)}, f32[512,1024]{1,0:T(8,128)}, ...) | async-done | bytes 16777232 | tf_op jit(solution)/shard_map/psum | solution.py:9
  365.6 0.0 copy-start.6
  365.6 10.4 %subtract_dynamic-update-slice_fusion = f32[8192,1024]{1,0:T(8,128)} fusion(f32[8192,1024]{1,0:T(8,128)} %copy.20, f32[512,1024]{1,0:T(8,128)} %get-tuple-element.5, f32[512,1024]{1,0:T(8,128)S(1)} %get-tuple-element.14), kind=kOutput, calls=%fused_computation.18 | convolution fusion | flops 6443499520 | bytes 12582912 | tf_op jit(solution)/shard_map/dot_general | solution.py:32
  376.0 0.0 copy-done.6
  376.0 0.0 copy-start.5
  376.0 10.1 %fusion.6 = f32[8192,1024]{1,0:T(8,128)} fusion(f32[8192,1024]{1,0:T(8,128)} %subtract_dynamic-update-slice_fusion, f32[512,1024]{1,0:T(8,128)S(1)} %copy-done.6, f32[512,1024]{1,0:T(8,128)S(1)} %get-tuple-element.14), kind=kOutput, calls=%fused_computation.13 | convolution fusion | flops 6443499520 | bytes 12582912 | tf_op jit(solution)/shard_map/dot_general | solution.py:32
  386.1 0.0 copy-done.5
  386.1 0.0 copy-start.4
  386.1 10.2 %fusion.5 = f32[8192,1024]{1,0:T(8,128)} fusion(f32[8192,1024]{1,0:T(8,128)} %fusion.6, f32[512,1024]{1,0:T(8,128)S(1)} %copy-done.5, f32[512,1024]{1,0:T(8,128)S(1)} %get-tuple-element.14), kind=kOutput, calls=%fused_computation.11 | convolution fusion | flops 6443499520 | bytes 12582912 | tf_op jit(solution)/shard_map/dot_general | solution.py:32
  396.3 0.0 copy-done.4
  396.3 0.0 copy-start.3
  396.3 10.1 %fusion.4 = f32[8192,1024]{1,0:T(8,128)} fusion(f32[8192,1024]{1,0:T(8,128)} %fusion.5, f32[512,1024]{1,0:T(8,128)S(1)} %copy-done.4, f32[512,1024]{1,0:T(8,128)S(1)} %get-tuple-element.14), kind=kOutput, calls=%fused_computation.9 | convolution fusion | flops 6443499520 | bytes 12582912 | tf_op jit(solution)/shard_map/dot_general | solution.py:32
  406.4 0.0 copy-done.3
  406.4 0.0 copy-start.2
  406.4 10.1 %fusion.3 = f32[8192,1024]{1,0:T(8,128)} fusion(f32[8192,1024]{1,0:T(8,128)} %fusion.4, f32[512,1024]{1,0:T(8,128)S(1)} %copy-done.3, f32[512,1024]{1,0:T(8,128)S(1)} %get-tuple-element.14), kind=kOutput, calls=%fused_computation.7 | convolution fusion | flops 6443499520 | bytes 12582912 | tf_op jit(solution)/shard_map/dot_general | solution.py:32
  416.5 0.0 copy-done.2
  416.5 0.0 copy-start.1
  416.5 10.3 %fusion.2 = f32[8192,1024]{1,0:T(8,128)} fusion(f32[8192,1024]{1,0:T(8,128)} %fusion.3, f32[512,1024]{1,0:T(8,128)S(1)} %copy-done.2, f32[512,1024]{1,0:T(8,128)S(1)} %get-tuple-element.14), kind=kOutput, calls=%fused_computation.5 | convolution fusion | flops 6443499520 | bytes 12582912 | tf_op jit(solution)/shard_map/dot_general | solution.py:32
  426.8 0.0 copy-done.1
  426.8 0.0 copy-start
  426.8 10.1 %fusion.1 = f32[8192,1024]{1,0:T(8,128)} fusion(f32[8192,1024]{1,0:T(8,128)} %fusion.2, f32[512,1024]{1,0:T(8,128)S(1)} %copy-done.1, f32[512,1024]{1,0:T(8,128)S(1)} %get-tuple-element.14), kind=kOutput, calls=%fused_computation.3 | convolution fusion | flops 6443499520 | bytes 12582912 | tf_op jit(solution)/shard_map/dot_general | solution.py:32
  436.9 0.0 copy-done
  436.9 9.9 %fusion = f32[8192,1024]{1,0:T(8,128)} fusion(f32[8192,1024]{1,0:T(8,128)} %fusion.1, f32[512,1024]{1,0:T(8,128)S(1)} %copy-done, f32[512,1024]{1,0:T(8,128)S(1)} %get-tuple-element.14), kind=kOutput, calls=%fused_computation.1 | convolution fusion | flops 6443499520 | bytes 12582912 | tf_op jit(solution)/shard_map/dot_general | solution.py:32
Async XLA Ops:
  6.5 23.5 %copy-start.7 = (f32[256,1024]{1,0:T(8,128)S(1)}, f32[256,1024]{1,0:T(8,128)}, u32[]{:S(2)}) copy-start(f32[256,1024]{1,0:T(8,128)} %param.2) | copy-start | bytes 3145732
  6.5 359.1 %all-reduce.3.cloned.1.call-start = ((), (), s32[]{:S(2)}) async-start(), calls=%async_computation | async-start | bytes 33554432 | tf_op jit(solution)/shard_map/psum | solution.py:9
  30.1 26.3 %collective-permute-start = (f32[256,1024]{1,0:T(8,128)S(1)}, f32[256,1024]{1,0:T(8,128)}, u32[]{:S(2)}, u32[]{:S(2)}) collective-permute-start(f32[256,1024]{1,0:T(8,128)S(1)} %copy-done.7), channel_id=1, source_target_pairs={{0,16},{16,0},{1,17},{17,1},{2,18},{18,2},{3,19},{19,3},{4,20},{20... | collective-permute-start | bytes 3145736 | tf_op jit(solution)/shard_map/ppermute | solution.py:18
  365.6 10.4 %copy-start.6 = (f32[512,1024]{1,0:T(8,128)S(1)}, f32[512,1024]{1,0:T(8,128)}, u32[]{:S(2)}) copy-start(f32[512,1024]{1,0:T(8,128)} %get-tuple-element.6) | copy-start | bytes 6291460
  376.0 10.1 %copy-start.5 = (f32[512,1024]{1,0:T(8,128)S(1)}, f32[512,1024]{1,0:T(8,128)}, u32[]{:S(2)}) copy-start(f32[512,1024]{1,0:T(8,128)} %get-tuple-element.7) | copy-start | bytes 6291460
  386.1 10.2 %copy-start.4 = (f32[512,1024]{1,0:T(8,128)S(1)}, f32[512,1024]{1,0:T(8,128)}, u32[]{:S(2)}) copy-start(f32[512,1024]{1,0:T(8,128)} %get-tuple-element.8) | copy-start | bytes 6291460
  396.3 10.1 %copy-start.3 = (f32[512,1024]{1,0:T(8,128)S(1)}, f32[512,1024]{1,0:T(8,128)}, u32[]{:S(2)}) copy-start(f32[512,1024]{1,0:T(8,128)} %get-tuple-element.9) | copy-start | bytes 6291460
  406.4 10.1 %copy-start.2 = (f32[512,1024]{1,0:T(8,128)S(1)}, f32[512,1024]{1,0:T(8,128)}, u32[]{:S(2)}) copy-start(f32[512,1024]{1,0:T(8,128)} %get-tuple-element.10) | copy-start | bytes 6291460
  416.5 10.3 %copy-start.1 = (f32[512,1024]{1,0:T(8,128)S(1)}, f32[512,1024]{1,0:T(8,128)}, u32[]{:S(2)}) copy-start(f32[512,1024]{1,0:T(8,128)} %get-tuple-element.11) | copy-start | bytes 6291460
  426.8 10.1 %copy-start = (f32[512,1024]{1,0:T(8,128)S(1)}, f32[512,1024]{1,0:T(8,128)}, u32[]{:S(2)}) copy-start(f32[512,1024]{1,0:T(8,128)} %get-tuple-element.12) | copy-start | bytes 6291460
Sparse Core Ops, SparseCore 0:
  65.8 299.7 all-reduce.2
